TPU v7x, 32 devices: a whole 2x2x4 slice. The times are simulated.
32 devices in a mesh: seq: 8 (over z, x), head: 4 (over y, core).
Axes of the slice: x: 2, y: 2, z: 4, core: 2. Of those that a mesh axis runs over, the one named last changes fastest.
Arguments:
- features: bfloat16 [8192, 8192], P(('seq', 'head')), may hold values from -6 to 6
- gate_input: bfloat16 [8192, 8192], P(('seq', 'head')), may hold values from -6 to 6
- bmat: bfloat16 [8192, 8, 128], P(('seq', 'head')), may hold values from -1.78125 to 1.78125
- cmat: bfloat16 [8192, 8, 128], P(('seq', 'head')), may hold values from -1.78125 to 1.78125
- step_size: float32 [8192, 128], P(('seq', 'head')), may hold values from 0.001 to 0.1
- log_decay: float32 [8192, 128], P(('seq', 'head')), may hold values from -0.8 to 0
- skip: float32 [128], P('head'), may hold values from 0.5 to 2
- norm_gain: float32 [8192], replicated, may hold values from 0.1 to 1.9
Outputs:
- mixed: bfloat16 [8192, 8192], P(('seq', 'head'))
All inputs are finite; a program needn't handle non-finite values.
Results may differ from a plain program's by a relative error of at most 0.0085.
Values may be sent and summed in bfloat16 or wider, within the bound.
No kernel may reach another device: no remote copies, remote signals or barrier semaphores. Data moves between devices by JAX's collectives and lax.ppermute only.
A program may use at most 128 MiB of HBM per device.

v0:
```python
import jax
import jax.numpy as jnp
from jax import lax
from jax.sharding import PartitionSpec as P

SPAN = 256


def passed_along(value, axis, steps):
    count = lax.axis_size(axis)
    leading, last = (max(0, -steps), min(count, count - steps))
    return lax.ppermute(value, axis, [(source, source + steps) for source in range(leading, last)])


def block_terms(feature_block, b_block, c_block, dt_block, cum_block):
    length = cum_block.shape[0]
    token_positions = jnp.arange(length)
    causal = token_positions[:, None] >= token_positions[None, :]
    scores = jnp.einsum("tgn,sgn->gts", c_block, b_block, preferred_element_type=jnp.float32)
    cum_heads = jnp.transpose(cum_block, (1, 2, 0))
    spread = cum_heads[:, :, :, None] - cum_heads[:, :, None, :]
    step_scale = jnp.transpose(dt_block, (1, 2, 0))[:, :, None, :]
    weights = jnp.where(
        causal, scores[:, None] * jnp.exp(jnp.where(causal, spread, 0.0)) * step_scale, 0.0
    ).astype(jnp.bfloat16)
    intra_terms = jnp.einsum(
        "ghts,sghp->tghp", weights, feature_block, preferred_element_type=jnp.float32
    )
    tail_scale = jnp.exp(cum_block[-1:] - cum_block) * dt_block
    loaded = (b_block[:, :, None, :].astype(jnp.float32) * tail_scale[..., None]).astype(
        jnp.bfloat16
    )
    update = jnp.einsum(
        "sghn,sghp->ghpn", loaded, feature_block, preferred_element_type=jnp.float32
    )
    return (intra_terms, update)


def normalize(values, gate_part, gain_row):
    gated_values = values.astype(jnp.float32) * jax.nn.silu(gate_part.astype(jnp.float32))
    inverse_rms = lax.rsqrt(jnp.mean(gated_values * gated_values, axis=-1, keepdims=True) + 1e-05)
    return (gated_values * inverse_rms * gain_row).astype(jnp.bfloat16)


def pair_terms(members):
    return jax.vmap(block_terms)(*members)


def shards(features, gate_input, bmat, cmat, step_size, log_decay, skip, norm_gain):
    tok_rows = features.shape[0]
    group_count = bmat.shape[1]
    state_size = bmat.shape[2]
    heads_total = step_size.shape[1]
    per_group = heads_total // group_count
    group_width = features.shape[1] // group_count
    head_size = group_width // per_group
    feature_groups = features.reshape(tok_rows, group_count, group_width)
    gate_groups = gate_input.reshape(tok_rows, group_count, group_width)
    dt_groups = step_size.reshape(tok_rows, group_count, per_group)
    decay_groups = log_decay.reshape(tok_rows, group_count, per_group)
    feature_here, gate_here, b_here, c_here = (
        lax.all_to_all(feature_groups, "head", split_axis=1, concat_axis=0, tiled=True),
        lax.all_to_all(gate_groups, "head", split_axis=1, concat_axis=0, tiled=True),
        lax.all_to_all(bmat, "head", split_axis=1, concat_axis=0, tiled=True),
        lax.all_to_all(cmat, "head", split_axis=1, concat_axis=0, tiled=True),
    )
    dt_here, decay_here = (
        lax.all_to_all(dt_groups, "head", split_axis=1, concat_axis=0, tiled=True),
        lax.all_to_all(decay_groups, "head", split_axis=1, concat_axis=0, tiled=True),
    )
    seq_rows = feature_here.shape[0]
    local_groups = feature_here.shape[1]
    blocks = seq_rows // SPAN
    feature_blocks = feature_here.reshape(blocks, SPAN, local_groups, per_group, head_size)
    b_blocks = b_here.reshape(blocks, SPAN, local_groups, state_size)
    c_blocks = c_here.reshape(blocks, SPAN, local_groups, state_size)
    dt_blocks = dt_here.reshape(blocks, SPAN, local_groups, per_group)
    decay_blocks = decay_here.reshape(blocks, SPAN, local_groups, per_group)
    cum_blocks = jnp.cumsum(decay_blocks, axis=1)

    def paired(array):
        return array.reshape((blocks // 2, 2) + array.shape[1:])

    intra_terms, updates = lax.map(
        pair_terms,
        (
            paired(feature_blocks),
            paired(b_blocks),
            paired(c_blocks),
            paired(dt_blocks),
            paired(cum_blocks),
        ),
    )
    intra_terms = intra_terms.reshape(blocks, SPAN, local_groups, per_group, head_size)
    updates = updates.reshape(blocks, local_groups, per_group, head_size, state_size)
    block_decay = jnp.exp(cum_blocks[:, -1])

    def advance(carry_state, members):
        decay_now, update_now = members
        return (decay_now[..., None, None] * carry_state + update_now, carry_state)

    start_state = jnp.zeros((local_groups, per_group, head_size, state_size), jnp.float32)
    local_end, local_states = lax.scan(advance, start_state, (block_decay, updates))
    block_sums = jnp.sum(decay_blocks, axis=1)
    before = jnp.cumsum(block_sums, axis=0) - block_sums
    shard_decay = jnp.exp(jnp.sum(block_sums, axis=0))

    def hop(iteration, incoming):
        return passed_along(shard_decay[..., None, None] * incoming + local_end, "seq", 1)

    entering = lax.fori_loop(0, lax.axis_size("seq") - 1, hop, jnp.zeros_like(local_end))
    states = local_states + jnp.exp(before)[..., None, None] * entering[None]
    carried = (
        jnp.einsum(
            "ktgn,kghpn->ktghp",
            c_blocks.astype(jnp.float32),
            states,
            precision=lax.Precision.HIGHEST,
        )
        * jnp.exp(cum_blocks)[..., None]
    )
    head_skip = skip.reshape(local_groups, per_group)
    ssm_out = (
        intra_terms
        + carried
        + head_skip[None, None, :, :, None] * feature_blocks.astype(jnp.float32)
    ).astype(jnp.bfloat16)
    ssm_out = ssm_out.reshape(seq_rows, local_groups, group_width)
    offset = lax.axis_index("head") * (local_groups * group_width)
    gain_here = lax.dynamic_slice_in_dim(norm_gain, offset, local_groups * group_width).reshape(
        local_groups, group_width
    )
    mixed_here = normalize(ssm_out, gate_here, gain_here)
    restored = lax.all_to_all(mixed_here, "head", split_axis=0, concat_axis=1, tiled=True)
    return restored.reshape(tok_rows, features.shape[1])


def solution(mesh):
    return jax.shard_map(
        shards,
        mesh=mesh,
        in_specs=(
            P(("seq", "head"), None),
            P(("seq", "head"), None),
            P(("seq", "head"), None, None),
            P(("seq", "head"), None, None),
            P(("seq", "head"), None),
            P(("seq", "head"), None),
            P("head"),
            P(),
        ),
        out_specs=P(("seq", "head"), None),
        check_vma=False,
    )
```

profile of v0, /device:TPU:8, one launch (start us, length us, event | category | flops | bytes accessed | tf_op | source)
XLA Modules:
  0.0 477.8 jit_solution(16098080593060179614)
XLA Ops:
  0.0 1.7 copy.123
  1.7 3.3 all-to-all-start.3
  5.0 1.6 copy.128
  6.6 2.9 all-to-all-done.3
  9.6 3.3 all-to-all-start.4
  12.9 1.9 copy.121
  14.8 2.6 all-to-all-done.4
  17.5 4.1 all-to-all-start.1
  21.6 6.4 %copy.118 = bf16[256,8192]{0,1:T(8,128)(2,1)} copy(bf16[256,8192]{1,0:T(8,128)(2,1)} %param.14) | data formatting | bytes 8388608 | tf_op args[0]
  28.0 6.5 %copy.119 = bf16[256,8,1024]{2,0,1:T(8,128)(2,1)} copy(bf16[256,8,1024]{0,2,1:T(8,128)(2,1)} %bitcast.164) | data formatting | bytes 8388608 | tf_op jit(solution)/shard_map/reshape | solution.py:57
  34.5 5.0 %all-to-all-start = ((bf16[256,8,1024]{2,0,1:T(8,128)(2,1)}), bf16[256,8,1024]{2,0,1:T(8,128)(2,1)}, u32[]{:S(2)}, u32[]{:S(2)}) async-start(bf16[256,8,1024]{2,0,1:T(8,128)(2,1)} %copy.119), calls=%async_computation | async-start | bytes 8388608 | tf_op jit(solution)/shard_map/all_to_all | solution.py:62
  39.6 0.9 copy.122
  40.4 6.4 %copy.132 = bf16[256,8192]{0,1:T(8,128)(2,1)} copy(bf16[256,8192]{1,0:T(8,128)(2,1)} %param.15) | data formatting | bytes 8388608 | tf_op args[1]
  46.9 0.7 dynamic_slice.29
  48.2 4.6 reduce-window.6
  53.3 34.5 %all-to-all-done = bf16[256,8,1024]{2,0,1:T(8,128)(2,1)} async-done(((bf16[256,8,1024]{2,0,1:T(8,128)(2,1)}), bf16[256,8,1024]{2,0,1:T(8,128)(2,1)}, u32[]{:S(2)}, u32[]{:S(2)}) %all-to-all-start) | async-done | bytes 4194336 | tf_op jit(solution)/shard_map/all_to_all | solution.py:62
  87.7 3.5 all-to-all-start.2
  91.5 6.2 %copy.120 = bf16[256,4,2,1024]{0,3,2,1:T(8,128)(2,1)} copy(bf16[256,4,2,1024]{3,0,2,1:T(8,128)(2,1)} %bitcast.13) | data formatting | bytes 8388608 | tf_op jit(solution)/shard_map/all_to_all | solution.py:62
  97.8 2.2 all-to-all-done.2
  100.0 5.0 %all-to-all-start.5 = ((bf16[256,8,1024]{0,2,1:T(8,128)(2,1)}), bf16[256,8,1024]{0,2,1:T(8,128)(2,1)}, u32[]{:S(2)}, u32[]{:S(2)}) async-start(bf16[256,8,1024]{0,2,1:T(8,128)(2,1)} %bitcast.161), calls=%async_computation.5 | async-start | bytes 8388608 | tf_op jit(solution)/shard_map/all_to_all | solution.py:63
  105.0 31.4 %while.35 = (s32[]{:T(128)}, f32[2,2,256,2,16,64]{2,5,4,3,1,0:T(8,128)}, f32[2,2,2,16,64,128]{5,4,3,2,1,0:T(8,128)}, bf16[2,2,256,2,16,64]{2,5,4,3,1,0:T(8,128)(...) while((s32[]{:T(128)}, ...), condition=%wide.region_3.4_spmd, body=%wide.region_2.3_spmd.sunk | while | flops 902004736 | bytes 15929189 | solution.py:84
  106.3 1.3 fusion.52
  107.6 7.3 %bitcast_dynamic-update-slice_fusion.6 = f32[2,2,256,2,16,64]{2,5,4,3,1,0:T(8,128)} fusion(f32[2,2,256,2,16,64]{2,5,4,3,1,0:T(8,128)} %get-tuple-element.328, s32[]{:T(128)} %get-tuple-element.327, f32[2,2,16,256]{3,2,1,0:T(8,128)S(1)} %copy.162, f32[2,2,16,256]{3,2,1,0:T(8,128)S(1)} %copy.164, f32[2,2,256,256]{3,2,1,0:T(8,128)S(1)} %fusion.52, ...), kind=kOutput, calls=%fused_computation.10.clone.1 | convolution fusion | flops 562036736 | bytes 7603200 | tf_op jit(solution)/shard_map/while/body/eval_jaxpr/vmap(ghts,sghp->tghp)/dot_general | solution.py:26
  115.6 5.1 %bitcast_dynamic-update-slice_fusion.7 = f32[2,2,2,16,64,128]{5,4,3,2,1,0:T(8,128)} fusion(f32[2,2,2,16,64,128]{5,4,3,2,1,0:T(8,128)} %get-tuple-element.329, s32[]{:T(128)} %get-tuple-element.327, f32[2,256,2,16]{1,3,2,0:T(8,128)S(1)} %copy.165, f32[2,256,2,128]{3,1,2,0:T(8,128)S(1)} %bitcast_convert_fusion.2, ...), kind=kOutput, calls=%fused_computation.13.clone.1 | convolution fusion | flops 272629760 | bytes 4785152 | tf_op jit(solution)/shard_map/while/body/eval_jaxpr/vmap(sghn,sghp->ghpn)/dot_general | solution.py:33
  122.0 1.3 fusion.52
  123.3 7.3 %bitcast_dynamic-update-slice_fusion.6 = f32[2,2,256,2,16,64]{2,5,4,3,1,0:T(8,128)} fusion(f32[2,2,256,2,16,64]{2,5,4,3,1,0:T(8,128)} %get-tuple-element.328, s32[]{:T(128)} %get-tuple-element.327, f32[2,2,16,256]{3,2,1,0:T(8,128)S(1)} %copy.162, f32[2,2,16,256]{3,2,1,0:T(8,128)S(1)} %copy.164, f32[2,2,256,256]{3,2,1,0:T(8,128)S(1)} %fusion.52, ...), kind=kOutput, calls=%fused_computation.10.clone.1 | convolution fusion | flops 562036736 | bytes 7603200 | tf_op jit(solution)/shard_map/while/body/eval_jaxpr/vmap(ghts,sghp->tghp)/dot_general | solution.py:26
  131.3 5.1 %bitcast_dynamic-update-slice_fusion.7 = f32[2,2,2,16,64,128]{5,4,3,2,1,0:T(8,128)} fusion(f32[2,2,2,16,64,128]{5,4,3,2,1,0:T(8,128)} %get-tuple-element.329, s32[]{:T(128)} %get-tuple-element.327, f32[2,256,2,16]{1,3,2,0:T(8,128)S(1)} %copy.165, f32[2,256,2,128]{3,1,2,0:T(8,128)S(1)} %bitcast_convert_fusion.2, ...), kind=kOutput, calls=%fused_computation.13.clone.1 | convolution fusion | flops 272629760 | bytes 4785152 | tf_op jit(solution)/shard_map/while/body/eval_jaxpr/vmap(sghn,sghp->ghpn)/dot_general | solution.py:33
  136.5 10.0 %while.37 = (s32[]{:T(128)}, f32[2,16,64,128]{3,2,1,0:T(8,128)S(1)}, f32[4,2,16,64,128]{4,3,2,1,0:T(8,128)}, f32[4,2,16]{2,1,0:T(2,128)S(1)}, f32[4,2,16,64,128]{4,3,2,1,0:T(8,128)}, /*index=5*/s32[]{:T(128)}, s32[]{:T(128)}) while((s32[]{:T(128)}, f32[2,16,64,128]{3,2,1,0:T(8,128)S(1)}, f32[4,2,16,64,128]{4,3,2,1,0:T(8,128)}, ...), condition=%wide.region_5.6_spmd.clone, body=%wide.region_4.5_spmd.clone.sunk | while | flops 1048579 | bytes 5243872 | solution.py:103
  136.5 1.1 bitcast_dynamic-update-slice_fusion.8
  137.6 1.4 bitcast_add_fusion.2
  139.0 1.0 bitcast_dynamic-update-slice_fusion.8
  140.0 1.4 bitcast_add_fusion.2
  141.5 1.1 bitcast_dynamic-update-slice_fusion.8
  142.5 1.4 bitcast_add_fusion.2
  144.0 1.1 bitcast_dynamic-update-slice_fusion.8
  145.0 1.4 bitcast_add_fusion.2
  146.5 6.6 %all-to-all-done.5 = bf16[256,8,1024]{0,2,1:T(8,128)(2,1)} async-done(((bf16[256,8,1024]{0,2,1:T(8,128)(2,1)}), bf16[256,8,1024]{0,2,1:T(8,128)(2,1)}, u32[]{:S(2)}, u32[]{:S(2)}) %all-to-all-start.5) | async-done | bytes 4194336 | tf_op jit(solution)/shard_map/all_to_all | solution.py:63
  153.0 6.2 %convert_element_type.75 = f32[256,8,1024]{0,2,1:T(8,128)} convert(bf16[256,8,1024]{0,2,1:T(8,128)(2,1)} %all-to-all-done.5) | non-fusion elementwise | flops 2097152 | bytes 12582912 | tf_op jit(solution)/shard_map/convert_element_type | solution.py:40
  159.3 175.0 %while.36 = (s32[]{:T(128)}, f32[2,16,64,128]{3,2,1,0:T(8,128)S(1)}, f32[2,16]{1,0:T(2,128)S(1)}, f32[2,16,64,128]{3,2,1,0:T(8,128)S(1)}, s32[]{:T(128)}) while((s32[]{:T(128)}, f32[2,16,64,128]{3,2,1,0:T(8,128)S(1)}, f32[2,16]{1,0:T(2,128)S(1)}, f32[2,16,64,128]{3,2,1,0:T(8,128)S(1)}, s32[]{:T(128)}) %tuple.65), condition=%wide.region_10.11_spmd, body=%wide.region_9.10_spmd.sunk | while | flops 524290 | bytes 7340261 | solution.py:111
  159.5 3.4 collective-permute-start
  162.9 24.0 %collective-permute-done = f32[2,16,64,128]{3,2,1,0:T(8,128)S(1)} collective-permute-done((f32[2,16,64,128]{3,2,1,0:T(8,128)S(1)}, f32[2,16,64,128]{3,2,1,0:T(8,128)S(1)}, u32[]{:S(2)}, u32[]{:S(2)}) %collective-permute-start) | collective-permute-done | bytes 1048608 | tf_op jit(solution)/shard_map/while/body/eval_jaxpr/ppermute | solution.py:12
  187.1 2.5 collective-permute-start
  189.6 24.0 %collective-permute-done = f32[2,16,64,128]{3,2,1,0:T(8,128)S(1)} collective-permute-done((f32[2,16,64,128]{3,2,1,0:T(8,128)S(1)}, f32[2,16,64,128]{3,2,1,0:T(8,128)S(1)}, u32[]{:S(2)}, u32[]{:S(2)}) %collective-permute-start) | collective-permute-done | bytes 1048608 | tf_op jit(solution)/shard_map/while/body/eval_jaxpr/ppermute | solution.py:12
  213.8 1.9 collective-permute-start
  215.7 23.8 %collective-permute-done = f32[2,16,64,128]{3,2,1,0:T(8,128)S(1)} collective-permute-done((f32[2,16,64,128]{3,2,1,0:T(8,128)S(1)}, f32[2,16,64,128]{3,2,1,0:T(8,128)S(1)}, u32[]{:S(2)}, u32[]{:S(2)}) %collective-permute-start) | collective-permute-done | bytes 1048608 | tf_op jit(solution)/shard_map/while/body/eval_jaxpr/ppermute | solution.py:12
  239.6 1.9 collective-permute-start
  241.6 22.9 %collective-permute-done = f32[2,16,64,128]{3,2,1,0:T(8,128)S(1)} collective-permute-done((f32[2,16,64,128]{3,2,1,0:T(8,128)S(1)}, f32[2,16,64,128]{3,2,1,0:T(8,128)S(1)}, u32[]{:S(2)}, u32[]{:S(2)}) %collective-permute-start) | collective-permute-done | bytes 1048608 | tf_op jit(solution)/shard_map/while/body/eval_jaxpr/ppermute | solution.py:12
  264.6 1.9 collective-permute-start
  266.6 22.0 %collective-permute-done = f32[2,16,64,128]{3,2,1,0:T(8,128)S(1)} collective-permute-done((f32[2,16,64,128]{3,2,1,0:T(8,128)S(1)}, f32[2,16,64,128]{3,2,1,0:T(8,128)S(1)}, u32[]{:S(2)}, u32[]{:S(2)}) %collective-permute-start) | collective-permute-done | bytes 1048608 | tf_op jit(solution)/shard_map/while/body/eval_jaxpr/ppermute | solution.py:12
  288.8 1.9 collective-permute-start
  290.7 21.2 %collective-permute-done = f32[2,16,64,128]{3,2,1,0:T(8,128)S(1)} collective-permute-done((f32[2,16,64,128]{3,2,1,0:T(8,128)S(1)}, f32[2,16,64,128]{3,2,1,0:T(8,128)S(1)}, u32[]{:S(2)}, u32[]{:S(2)}) %collective-permute-start) | collective-permute-done | bytes 1048608 | tf_op jit(solution)/shard_map/while/body/eval_jaxpr/ppermute | solution.py:12
  312.1 1.9 collective-permute-start
  314.0 20.3 %collective-permute-done = f32[2,16,64,128]{3,2,1,0:T(8,128)S(1)} collective-permute-done((f32[2,16,64,128]{3,2,1,0:T(8,128)S(1)}, f32[2,16,64,128]{3,2,1,0:T(8,128)S(1)}, u32[]{:S(2)}, u32[]{:S(2)}) %collective-permute-start) | collective-permute-done | bytes 1048608 | tf_op jit(solution)/shard_map/while/body/eval_jaxpr/ppermute | solution.py:12
  334.4 13.8 %multiply_reduce_fusion = (f32[4,256,2]{1,2,0:T(2,128)S(1)}, f32[4,256,2,16,64]{1,4,3,2,0:T(8,128)}) fusion(f32[4,256,2,16,64]{1,4,3,2,0:T(8,128)} %bitcast.157, bf16[4,256,2,16,64]{1,4,3,2,0:T(8,128)(2,1)} %bitcast.167, f32[2,16]{1,0:T(2,128)S(1)} %mul.128, f32[4,256,2,16]{1,3,2,0:T(8,128)S(1)} %bitcast_exponential_fusion, ...), kind=kOutput, calls=%fused_computation.43 | convolution fusion | flops 3252680704 | bytes 35267200 | tf_op jit(solution)/shard_map/ktgn,kghpn->ktghp/dot_general | solution.py:114
  348.2 13.8 %copy.131 = f32[4,256,2,16,64]{1,0,4,3,2:T(4,128)} copy(f32[4,256,2,16,64]{1,4,3,2,0:T(8,128)} %get-tuple-element.208) | data formatting | bytes 16777216 | tf_op jit(solution)/shard_map/convert_element_type | solution.py:40
  361.9 10.7 %reshape.131 = f32[1024,2,1024]{0,2,1:T(8,128)} reshape(f32[4,256,2,16,64]{1,0,4,3,2:T(4,128)} %copy.131) | data formatting | bytes 16777216 | tf_op jit(solution)/shard_map/convert_element_type | solution.py:40
  372.7 8.8 %copy.134 = f32[4,256,2,1024]{3,1,0,2:T(8,128)} copy(f32[4,256,2,1024]{1,3,2,0:T(8,128)} %bitcast.158) | data formatting | bytes 16777216 | tf_op jit(solution)/shard_map/convert_element_type | solution.py:40
  381.4 8.7 %copy.136 = f32[1024,2,1024]{0,2,1:T(8,128)} copy(f32[1024,2,1024]{2,0,1:T(8,128)} %bitcast.159) | data formatting | bytes 16777216 | tf_op jit(solution)/shard_map/convert_element_type | solution.py:40
  390.1 8.6 %multiply_convert_fusion.4 = bf16[1024,2,1024]{0,2,1:T(8,128)(2,1)} fusion(f32[1024,2,1024]{0,2,1:T(8,128)} %reshape.131, f32[1024,2,1024]{0,2,1:T(8,128)} %copy.136, f32[2,1024]{1,0:T(2,128)S(1)} %copy-done.1, f32[1024,2]{0,1:T(2,128)S(1)} %bitcast.174), kind=kLoop, calls=%fused_computation.42 | loop fusion | flops 16777216 | bytes 20987904 | tf_op jit(solution)/shard_map/convert_element_type | solution.py:42
  398.7 11.3 %copy.138 = bf16[1024,2,1024]{2,1,0:T(2,128)(2,1)} copy(bf16[1024,2,1024]{0,2,1:T(8,128)(2,1)} %multiply_convert_fusion.4) | data formatting | bytes 8388608 | tf_op jit(solution)/shard_map/convert_element_type | solution.py:42
  410.0 51.9 %all_to_all.96 = bf16[1024,2,1024]{2,1,0:T(2,128)(2,1)S(1)} all-to-all(bf16[1024,2,1024]{2,1,0:T(2,128)(2,1)} %copy.138), channel_id=1, replica_groups=mesh['seq'=8,'head'=4] {'head'}, dimensions={0} | all-to-all | bytes 8388608 | tf_op jit(solution)/shard_map/all_to_all | solution.py:134
  461.9 3.3 copy.139
  465.2 6.2 %copy.140 = bf16[256,4,2,1024]{0,3,2,1:T(8,128)(2,1)} copy(bf16[256,4,2,1024]{3,0,1,2:T(8,128)(2,1)} %bitcast.162) | data formatting | bytes 8388608 | tf_op jit(solution)/shard_map/all_to_all | solution.py:134
  471.5 6.3 %copy.141 = bf16[256,8192]{1,0:T(8,128)(2,1)} copy(bf16[256,8192]{0,1:T(8,128)(2,1)} %bitcast.163) | data formatting | bytes 8388608 | tf_op jit(solution)/shard_map/reshape | solution.py:135
  (59 shorter events, 6.6 us)
Async XLA Ops:
  1.7 7.9 %all-to-all-start.3 = ((f32[256,8,16]{0,2,1:T(8,128)}), f32[256,8,16]{0,2,1:T(8,128)S(1)}, u32[]{:S(2)}, u32[]{:S(2)}) async-start(f32[256,8,16]{0,2,1:T(8,128)} %bitcast.22), calls=%async_computation.3 | async-start | bytes 262144 | tf_op jit(solution)/shard_map/all_to_all | solution.py:69
  9.6 7.9 %all-to-all-start.4 = ((f32[256,8,16]{0,2,1:T(8,128)}), f32[256,8,16]{0,2,1:T(8,128)S(1)}, u32[]{:S(2)}, u32[]{:S(2)}) async-start(f32[256,8,16]{0,2,1:T(8,128)} %bitcast.28), calls=%async_computation.4 | async-start | bytes 262144 | tf_op jit(solution)/shard_map/all_to_all | solution.py:68
  17.5 17.1 %all-to-all-start.1 = ((bf16[256,8,128]{2,0,1:T(8,128)(2,1)}), bf16[256,8,128]{2,0,1:T(8,128)(2,1)}, u32[]{:S(2)}, u32[]{:S(2)}) async-start(bf16[256,8,128]{2,0,1:T(8,128)(2,1)} %copy.121), calls=%async_computation.1 | async-start | bytes 1048576 | tf_op jit(solution)/shard_map/all_to_all | solution.py:65
  28.0 11.6 %copy-start = (bf16[256,8,128]{2,1,0:T(8,128)(2,1)S(1)}, bf16[256,8,128]{2,1,0:T(8,128)(2,1)}, u32[]{:S(2)}) copy-start(bf16[256,8,128]{2,1,0:T(8,128)(2,1)} %param.16) | copy-start | bytes 1572868
  34.5 12.3 %copy-start.2 = (f32[32]{0:T(128)S(1)}, f32[32]{0:T(128)}, u32[]{:S(2)}) copy-start(f32[32]{0:T(128)} %param.20) | copy-start | bytes 388
  34.5 53.2 %all-to-all-start = ((bf16[256,8,1024]{2,0,1:T(8,128)(2,1)}), bf16[256,8,1024]{2,0,1:T(8,128)(2,1)}, u32[]{:S(2)}, u32[]{:S(2)}) async-start(bf16[256,8,1024]{2,0,1:T(8,128)(2,1)} %copy.119), calls=%async_computation | async-start | bytes 8388608 | tf_op jit(solution)/shard_map/all_to_all | solution.py:62
  87.7 12.3 %all-to-all-start.2 = ((bf16[256,8,128]{2,0,1:T(8,128)(2,1)}), bf16[256,8,128]{2,0,1:T(8,128)(2,1)S(1)}, u32[]{:S(2)}, u32[]{:S(2)}) async-start(bf16[256,8,128]{2,0,1:T(8,128)(2,1)} %copy.122), calls=%async_computation.2 | async-start | bytes 1048576 | tf_op jit(solution)/shard_map/all_to_all | solution.py:64
  100.0 53.1 %all-to-all-start.5 = ((bf16[256,8,1024]{0,2,1:T(8,128)(2,1)}), bf16[256,8,1024]{0,2,1:T(8,128)(2,1)}, u32[]{:S(2)}, u32[]{:S(2)}) async-start(bf16[256,8,1024]{0,2,1:T(8,128)(2,1)} %bitcast.161), calls=%async_computation.5 | async-start | bytes 8388608 | tf_op jit(solution)/shard_map/all_to_all | solution.py:63
  159.5 27.4 %collective-permute-start = (f32[2,16,64,128]{3,2,1,0:T(8,128)S(1)}, f32[2,16,64,128]{3,2,1,0:T(8,128)S(1)}, u32[]{:S(2)}, u32[]{:S(2)}) collective-permute-start(f32[2,16,64,128]{3,2,1,0:T(8,128)S(1)} %multiply_add_fusion.2), channel_id=1, source_target_pairs={{0,4},{4,8},{8,12},{12,16},{16,20},{20,24},{24,28},{1,5},{5,9},{9,... | collective-permute-start | bytes 3145736 | tf_op jit(solution)/shard_map/while/body/eval_jaxpr/ppermute | solution.py:12
  187.1 26.5 %collective-permute-start = (f32[2,16,64,128]{3,2,1,0:T(8,128)S(1)}, f32[2,16,64,128]{3,2,1,0:T(8,128)S(1)}, u32[]{:S(2)}, u32[]{:S(2)}) collective-permute-start(f32[2,16,64,128]{3,2,1,0:T(8,128)S(1)} %multiply_add_fusion.2), channel_id=1, source_target_pairs={{0,4},{4,8},{8,12},{12,16},{16,20},{20,24},{24,28},{1,5},{5,9},{9,... | collective-permute-start | bytes 3145736 | tf_op jit(solution)/shard_map/while/body/eval_jaxpr/ppermute | solution.py:12
  213.8 25.7 %collective-permute-start = (f32[2,16,64,128]{3,2,1,0:T(8,128)S(1)}, f32[2,16,64,128]{3,2,1,0:T(8,128)S(1)}, u32[]{:S(2)}, u32[]{:S(2)}) collective-permute-start(f32[2,16,64,128]{3,2,1,0:T(8,128)S(1)} %multiply_add_fusion.2), channel_id=1, source_target_pairs={{0,4},{4,8},{8,12},{12,16},{16,20},{20,24},{24,28},{1,5},{5,9},{9,... | collective-permute-start | bytes 3145736 | tf_op jit(solution)/shard_map/while/body/eval_jaxpr/ppermute | solution.py:12
  239.6 24.8 %collective-permute-start = (f32[2,16,64,128]{3,2,1,0:T(8,128)S(1)}, f32[2,16,64,128]{3,2,1,0:T(8,128)S(1)}, u32[]{:S(2)}, u32[]{:S(2)}) collective-permute-start(f32[2,16,64,128]{3,2,1,0:T(8,128)S(1)} %multiply_add_fusion.2), channel_id=1, source_target_pairs={{0,4},{4,8},{8,12},{12,16},{16,20},{20,24},{24,28},{1,5},{5,9},{9,... | collective-permute-start | bytes 3145736 | tf_op jit(solution)/shard_map/while/body/eval_jaxpr/ppermute | solution.py:12
  264.6 24.0 %collective-permute-start = (f32[2,16,64,128]{3,2,1,0:T(8,128)S(1)}, f32[2,16,64,128]{3,2,1,0:T(8,128)S(1)}, u32[]{:S(2)}, u32[]{:S(2)}) collective-permute-start(f32[2,16,64,128]{3,2,1,0:T(8,128)S(1)} %multiply_add_fusion.2), channel_id=1, source_target_pairs={{0,4},{4,8},{8,12},{12,16},{16,20},{20,24},{24,28},{1,5},{5,9},{9,... | collective-permute-start | bytes 3145736 | tf_op jit(solution)/shard_map/while/body/eval_jaxpr/ppermute | solution.py:12
  288.8 23.2 %collective-permute-start = (f32[2,16,64,128]{3,2,1,0:T(8,128)S(1)}, f32[2,16,64,128]{3,2,1,0:T(8,128)S(1)}, u32[]{:S(2)}, u32[]{:S(2)}) collective-permute-start(f32[2,16,64,128]{3,2,1,0:T(8,128)S(1)} %multiply_add_fusion.2), channel_id=1, source_target_pairs={{0,4},{4,8},{8,12},{12,16},{16,20},{20,24},{24,28},{1,5},{5,9},{9,... | collective-permute-start | bytes 3145736 | tf_op jit(solution)/shard_map/while/body/eval_jaxpr/ppermute | solution.py:12
  312.1 22.3 %collective-permute-start = (f32[2,16,64,128]{3,2,1,0:T(8,128)S(1)}, f32[2,16,64,128]{3,2,1,0:T(8,128)S(1)}, u32[]{:S(2)}, u32[]{:S(2)}) collective-permute-start(f32[2,16,64,128]{3,2,1,0:T(8,128)S(1)} %multiply_add_fusion.2), channel_id=1, source_target_pairs={{0,4},{4,8},{8,12},{12,16},{16,20},{20,24},{24,28},{1,5},{5,9},{9,... | collective-permute-start | bytes 3145736 | tf_op jit(solution)/shard_map/while/body/eval_jaxpr/ppermute | solution.py:12
  381.4 8.7 %copy-start.1 = (f32[2,1024]{1,0:T(2,128)S(1)}, f32[2,1024]{1,0:T(2,128)}, u32[]{:S(2)}) copy-start(f32[2,1024]{1,0:T(2,128)} %mul.139) | copy-start | bytes 24580
where the time goes:
time: 481 us; the launch traced here: 478 us
  waiting for transfers between devices  207 us (43%)
  local copies, waits for them, and re-layouts  106 us (22%)
  blocking collectives  51.9 us (11%)
  matrix products  41.3 us (9%)
  starting transfers between devices  39.8 us (8%)
  other arithmetic  31.6 us (7%)
    ppermute x7, waiting for transfers between devices, passed_along(): lax.ppermute(value, axis, [(source, source + steps) for source in range(l...  158 us
    all_to_all x1, blocking collectives, shards(): lax.all_to_all(mixed_here, 'head', split_axis=0, concat_axis=1, tiled=True)  51.9 us
    all_to_all x1, waiting for transfers between devices, shards(): lax.all_to_all(feature_groups, 'head', split_axis=1, concat_axis=0, tiled...  34.5 us
    convert_element_type x2, local copies, waits for them, and re-layouts, normalize(): values.astype(jnp.float32) * jax.nn.silu(gate_part.astype(jnp.float32))  24.5 us
    unnamed x12, local copies, waits for them, and re-layouts  18.8 us
    convert_element_type x2, local copies, waits for them, and re-layouts, normalize(): gate_part.astype(jnp.float32)  17.5 us
    ppermute x7, starting transfers between devices, passed_along(): lax.ppermute(value, axis, [(source, source + steps) for source in range(l...  15.5 us
    dot_general x2, matrix products, block_terms(): jnp.einsum('ghts,sghp->tghp', weights, feature_block, preferred_element_t...  14.7 us
  transfers between devices with their start and end apart: 13, of which 12 were waited for; matrix products, arithmetic and copies ran while one was open for 16% of the time, Pallas kernels for 0%

commit v1 on v0

--- a/solution.py
+++ b/solution.py
@@ -2,6 +2,7 @@
 import jax.numpy as jnp
 from jax import lax
 from jax.sharding import PartitionSpec as P
+from jax.lax import all_to_all, axis_size
 
 SPAN = 256
 
@@ -131,7 +132,15 @@
         local_groups, group_width
     )
     mixed_here = normalize(ssm_out, gate_here, gain_here)
-    restored = lax.all_to_all(mixed_here, "head", split_axis=0, concat_axis=1, tiled=True)
+    restored = jnp.concatenate(
+        all_to_all(
+            jnp.stack(jnp.split(mixed_here, axis_size("head"), axis=0)),
+            axis_name="head",
+            split_axis=0,
+            concat_axis=0,
+        ),
+        axis=1,
+    )
     return restored.reshape(tok_rows, features.shape[1])
 
 

time: 481 us -> 459 us (0.954)
  local copies, waits for them, and re-layouts: 106 us -> 85.2 us
    convert_element_type x1 -> x0, local copies, waits for them, and re-layouts: 11.3 us -> none  [normalize(): return (gated_values * inverse_rms * gain_row).astype(jnp.bfloat16)]
    all_to_all x2 -> x0, local copies, waits for them, and re-layouts: 9.56 us -> none  [shards(): lax.all_to_all(mixed_here, 'head', split_axis=0, concat_axis=1, tiled=True)]
    another operation x3 -> x5, local copies, waits for them, and re-layouts: 0.12 us -> 6.71 us  [the longest x1 6.32 us: shards(): return restored.reshape(tok_rows, features.shape[1])]
    reshape x2 -> x1, local copies, waits for them, and re-layouts: 6.32 us -> 0.01 us  [the longest x1 6.31 us: shards(): return restored.reshape(tok_rows, features.shape[1])]
  transfers between devices with their start and end apart: 13 -> 13, of which waited for: 12 -> 12; matrix products, arithmetic and copies ran while one was open for 16% -> 17% of each run, Pallas kernels for 0% -> 0%
where the time goes in v1:
time: 459 us; the launch traced here: 456 us
  waiting for transfers between devices  207 us (45%)
  local copies, waits for them, and re-layouts  85.2 us (19%)
  blocking collectives  51.5 us (11%)
  matrix products  41.2 us (9%)
  starting transfers between devices  39.8 us (9%)
  other arithmetic  30.9 us (7%)
    ppermute x7, waiting for transfers between devices, passed_along(): lax.ppermute(value, axis, [(source, source + steps) for source in range(l...  158 us
    all_to_all x1, blocking collectives, shards(): all_to_all(jnp.stack(jnp.split(mixed_here, axis_size('head'), axis=0)), a...  51.5 us
    all_to_all x1, waiting for transfers between devices, shards(): lax.all_to_all(feature_groups, 'head', split_axis=1, concat_axis=0, tiled...  34.4 us
    convert_element_type x2, local copies, waits for them, and re-layouts, normalize(): values.astype(jnp.float32) * jax.nn.silu(gate_part.astype(jnp.float32))  24.5 us
    unnamed x12, local copies, waits for them, and re-layouts  18.9 us
    convert_element_type x2, local copies, waits for them, and re-layouts, normalize(): gate_part.astype(jnp.float32)  17.4 us
    ppermute x7, starting transfers between devices, passed_along(): lax.ppermute(value, axis, [(source, source + steps) for source in range(l...  15.5 us
    dot_general x2, matrix products, block_terms(): jnp.einsum('ghts,sghp->tghp', weights, feature_block, preferred_element_t...  14.7 us
  transfers between devices with their start and end apart: 13, of which 12 were waited for; matrix products, arithmetic and copies ran while one was open for 17% of the time, Pallas kernels for 0%

profile of v1, /device:TPU:8, one launch (start us, length us, event | category | flops | bytes accessed | tf_op | source)
XLA Modules:
  0.0 456.1 jit_solution(14529890308424106190)
XLA Ops:
  0.0 1.7 copy.119
  1.7 3.3 all-to-all-start.3
  5.0 1.7 copy.124
  6.6 2.9 all-to-all-done.3
  9.6 3.3 all-to-all-start.4
  12.9 1.9 copy.117
  14.8 2.6 all-to-all-done.4
  17.5 4.2 all-to-all-start.1
  21.6 6.4 %copy.114 = bf16[256,8192]{0,1:T(8,128)(2,1)} copy(bf16[256,8192]{1,0:T(8,128)(2,1)} %param.14) | data formatting | bytes 8388608 | tf_op args[0]
  28.0 6.5 %copy.115 = bf16[256,8,1024]{2,0,1:T(8,128)(2,1)} copy(bf16[256,8,1024]{0,2,1:T(8,128)(2,1)} %bitcast.170) | data formatting | bytes 8388608 | tf_op jit(solution)/shard_map/reshape | solution.py:58
  34.5 5.0 %all-to-all-start = ((bf16[256,8,1024]{2,0,1:T(8,128)(2,1)}), bf16[256,8,1024]{2,0,1:T(8,128)(2,1)}, u32[]{:S(2)}, u32[]{:S(2)}) async-start(bf16[256,8,1024]{2,0,1:T(8,128)(2,1)} %copy.115), calls=%async_computation | async-start | bytes 8388608 | tf_op jit(solution)/shard_map/all_to_all | solution.py:63
  39.6 0.9 copy.118
  40.5 6.4 %copy.128 = bf16[256,8192]{0,1:T(8,128)(2,1)} copy(bf16[256,8192]{1,0:T(8,128)(2,1)} %param.15) | data formatting | bytes 8388608 | tf_op args[1]
  46.9 0.7 dynamic_slice.29
  47.6 0.6 mul.139
  48.2 4.6 reduce-window.6
  53.3 34.4 %all-to-all-done = bf16[256,8,1024]{2,0,1:T(8,128)(2,1)} async-done(((bf16[256,8,1024]{2,0,1:T(8,128)(2,1)}), bf16[256,8,1024]{2,0,1:T(8,128)(2,1)}, u32[]{:S(2)}, u32[]{:S(2)}) %all-to-all-start) | async-done | bytes 4194336 | tf_op jit(solution)/shard_map/all_to_all | solution.py:63
  87.7 3.5 all-to-all-start.2
  91.5 6.3 %copy.116 = bf16[256,4,2,1024]{0,3,2,1:T(8,128)(2,1)} copy(bf16[256,4,2,1024]{3,0,2,1:T(8,128)(2,1)} %bitcast.13) | data formatting | bytes 8388608 | tf_op jit(solution)/shard_map/all_to_all | solution.py:63
  97.8 2.1 all-to-all-done.2
  100.0 5.0 %all-to-all-start.5 = ((bf16[256,8,1024]{0,2,1:T(8,128)(2,1)}), bf16[256,8,1024]{0,2,1:T(8,128)(2,1)}, u32[]{:S(2)}, u32[]{:S(2)}) async-start(bf16[256,8,1024]{0,2,1:T(8,128)(2,1)} %bitcast.168), calls=%async_computation.5 | async-start | bytes 8388608 | tf_op jit(solution)/shard_map/all_to_all | solution.py:64
  105.0 31.4 %while.35 = (s32[]{:T(128)}, f32[2,2,256,2,16,64]{2,5,4,3,1,0:T(8,128)}, f32[2,2,2,16,64,128]{5,4,3,2,1,0:T(8,128)}, bf16[2,2,256,2,16,64]{2,5,4,3,1,0:T(8,128)(...) while((s32[]{:T(128)}, ...), condition=%wide.region_3.4_spmd, body=%wide.region_2.3_spmd.sunk | while | flops 902004736 | bytes 15929189 | solution.py:85
  106.3 1.3 fusion.52
  107.6 7.3 %bitcast_dynamic-update-slice_fusion.6 = f32[2,2,256,2,16,64]{2,5,4,3,1,0:T(8,128)} fusion(f32[2,2,256,2,16,64]{2,5,4,3,1,0:T(8,128)} %get-tuple-element.332, s32[]{:T(128)} %get-tuple-element.331, f32[2,2,16,256]{3,2,1,0:T(8,128)S(1)} %copy.155, f32[2,2,16,256]{3,2,1,0:T(8,128)S(1)} %copy.157, f32[2,2,256,256]{3,2,1,0:T(8,128)S(1)} %fusion.52, ...), kind=kOutput, calls=%fused_computation.10.clone.1 | convolution fusion | flops 562036736 | bytes 7603200 | tf_op jit(solution)/shard_map/while/body/eval_jaxpr/vmap(ghts,sghp->tghp)/dot_general | solution.py:27
  114.9 0.4 bitcast_multiply_fusion.3
  115.6 5.1 %bitcast_dynamic-update-slice_fusion.7 = f32[2,2,2,16,64,128]{5,4,3,2,1,0:T(8,128)} fusion(f32[2,2,2,16,64,128]{5,4,3,2,1,0:T(8,128)} %get-tuple-element.333, s32[]{:T(128)} %get-tuple-element.331, f32[2,256,2,16]{1,3,2,0:T(8,128)S(1)} %copy.158, f32[2,256,2,128]{3,1,2,0:T(8,128)S(1)} %bitcast_convert_fusion.2, ...), kind=kOutput, calls=%fused_computation.13.clone.1 | convolution fusion | flops 272629760 | bytes 4785152 | tf_op jit(solution)/shard_map/while/body/eval_jaxpr/vmap(sghn,sghp->ghpn)/dot_general | solution.py:34
  122.0 1.3 fusion.52
  123.3 7.3 %bitcast_dynamic-update-slice_fusion.6 = f32[2,2,256,2,16,64]{2,5,4,3,1,0:T(8,128)} fusion(f32[2,2,256,2,16,64]{2,5,4,3,1,0:T(8,128)} %get-tuple-element.332, s32[]{:T(128)} %get-tuple-element.331, f32[2,2,16,256]{3,2,1,0:T(8,128)S(1)} %copy.155, f32[2,2,16,256]{3,2,1,0:T(8,128)S(1)} %copy.157, f32[2,2,256,256]{3,2,1,0:T(8,128)S(1)} %fusion.52, ...), kind=kOutput, calls=%fused_computation.10.clone.1 | convolution fusion | flops 562036736 | bytes 7603200 | tf_op jit(solution)/shard_map/while/body/eval_jaxpr/vmap(ghts,sghp->tghp)/dot_general | solution.py:27
  131.3 5.1 %bitcast_dynamic-update-slice_fusion.7 = f32[2,2,2,16,64,128]{5,4,3,2,1,0:T(8,128)} fusion(f32[2,2,2,16,64,128]{5,4,3,2,1,0:T(8,128)} %get-tuple-element.333, s32[]{:T(128)} %get-tuple-element.331, f32[2,256,2,16]{1,3,2,0:T(8,128)S(1)} %copy.158, f32[2,256,2,128]{3,1,2,0:T(8,128)S(1)} %bitcast_convert_fusion.2, ...), kind=kOutput, calls=%fused_computation.13.clone.1 | convolution fusion | flops 272629760 | bytes 4785152 | tf_op jit(solution)/shard_map/while/body/eval_jaxpr/vmap(sghn,sghp->ghpn)/dot_general | solution.py:34
  136.4 10.0 %while.37 = (s32[]{:T(128)}, f32[2,16,64,128]{3,2,1,0:T(8,128)S(1)}, f32[4,2,16,64,128]{4,3,2,1,0:T(8,128)}, f32[4,2,16]{2,1,0:T(2,128)S(1)}, f32[4,2,16,64,128]{4,3,2,1,0:T(8,128)}, /*index=5*/s32[]{:T(128)}, s32[]{:T(128)}) while((s32[]{:T(128)}, f32[2,16,64,128]{3,2,1,0:T(8,128)S(1)}, f32[4,2,16,64,128]{4,3,2,1,0:T(8,128)}, ...), condition=%wide.region_5.6_spmd.clone, body=%wide.region_4.5_spmd.clone.sunk | while | flops 1048579 | bytes 5243872 | solution.py:104
  136.4 1.1 bitcast_dynamic-update-slice_fusion.8
  137.6 1.4 bitcast_add_fusion.2
  139.0 1.1 bitcast_dynamic-update-slice_fusion.8
  140.0 1.4 bitcast_add_fusion.2
  141.5 1.1 bitcast_dynamic-update-slice_fusion.8
  142.6 1.4 bitcast_add_fusion.2
  144.0 1.1 bitcast_dynamic-update-slice_fusion.8
  145.1 1.4 bitcast_add_fusion.2
  146.5 6.6 %all-to-all-done.5 = bf16[256,8,1024]{0,2,1:T(8,128)(2,1)} async-done(((bf16[256,8,1024]{0,2,1:T(8,128)(2,1)}), bf16[256,8,1024]{0,2,1:T(8,128)(2,1)}, u32[]{:S(2)}, u32[]{:S(2)}) %all-to-all-start.5) | async-done | bytes 4194336 | tf_op jit(solution)/shard_map/all_to_all | solution.py:64
  153.0 6.2 %convert_element_type.75 = f32[256,8,1024]{0,2,1:T(8,128)} convert(bf16[256,8,1024]{0,2,1:T(8,128)(2,1)} %all-to-all-done.5) | non-fusion elementwise | flops 2097152 | bytes 12582912 | tf_op jit(solution)/shard_map/convert_element_type | solution.py:41
  159.3 175.0 %while.36 = (s32[]{:T(128)}, f32[2,16,64,128]{3,2,1,0:T(8,128)S(1)}, f32[2,16]{1,0:T(2,128)S(1)}, f32[2,16,64,128]{3,2,1,0:T(8,128)S(1)}, s32[]{:T(128)}) while((s32[]{:T(128)}, f32[2,16,64,128]{3,2,1,0:T(8,128)S(1)}, f32[2,16]{1,0:T(2,128)S(1)}, f32[2,16,64,128]{3,2,1,0:T(8,128)S(1)}, s32[]{:T(128)}) %tuple.68), condition=%wide.region_10.11_spmd, body=%wide.region_9.10_spmd.sunk | while | flops 524290 | bytes 7340261 | solution.py:112
  159.5 3.4 collective-permute-start
  162.9 24.0 %collective-permute-done = f32[2,16,64,128]{3,2,1,0:T(8,128)S(1)} collective-permute-done((f32[2,16,64,128]{3,2,1,0:T(8,128)S(1)}, f32[2,16,64,128]{3,2,1,0:T(8,128)S(1)}, u32[]{:S(2)}, u32[]{:S(2)}) %collective-permute-start) | collective-permute-done | bytes 1048608 | tf_op jit(solution)/shard_map/while/body/eval_jaxpr/ppermute | solution.py:13
  187.1 2.5 collective-permute-start
  189.6 24.0 %collective-permute-done = f32[2,16,64,128]{3,2,1,0:T(8,128)S(1)} collective-permute-done((f32[2,16,64,128]{3,2,1,0:T(8,128)S(1)}, f32[2,16,64,128]{3,2,1,0:T(8,128)S(1)}, u32[]{:S(2)}, u32[]{:S(2)}) %collective-permute-start) | collective-permute-done | bytes 1048608 | tf_op jit(solution)/shard_map/while/body/eval_jaxpr/ppermute | solution.py:13
  213.8 1.9 collective-permute-start
  215.7 23.8 %collective-permute-done = f32[2,16,64,128]{3,2,1,0:T(8,128)S(1)} collective-permute-done((f32[2,16,64,128]{3,2,1,0:T(8,128)S(1)}, f32[2,16,64,128]{3,2,1,0:T(8,128)S(1)}, u32[]{:S(2)}, u32[]{:S(2)}) %collective-permute-start) | collective-permute-done | bytes 1048608 | tf_op jit(solution)/shard_map/while/body/eval_jaxpr/ppermute | solution.py:13
  239.6 1.9 collective-permute-start
  241.6 22.9 %collective-permute-done = f32[2,16,64,128]{3,2,1,0:T(8,128)S(1)} collective-permute-done((f32[2,16,64,128]{3,2,1,0:T(8,128)S(1)}, f32[2,16,64,128]{3,2,1,0:T(8,128)S(1)}, u32[]{:S(2)}, u32[]{:S(2)}) %collective-permute-start) | collective-permute-done | bytes 1048608 | tf_op jit(solution)/shard_map/while/body/eval_jaxpr/ppermute | solution.py:13
  264.6 1.9 collective-permute-start
  266.6 22.0 %collective-permute-done = f32[2,16,64,128]{3,2,1,0:T(8,128)S(1)} collective-permute-done((f32[2,16,64,128]{3,2,1,0:T(8,128)S(1)}, f32[2,16,64,128]{3,2,1,0:T(8,128)S(1)}, u32[]{:S(2)}, u32[]{:S(2)}) %collective-permute-start) | collective-permute-done | bytes 1048608 | tf_op jit(solution)/shard_map/while/body/eval_jaxpr/ppermute | solution.py:13
  288.8 1.9 collective-permute-start
  290.7 21.2 %collective-permute-done = f32[2,16,64,128]{3,2,1,0:T(8,128)S(1)} collective-permute-done((f32[2,16,64,128]{3,2,1,0:T(8,128)S(1)}, f32[2,16,64,128]{3,2,1,0:T(8,128)S(1)}, u32[]{:S(2)}, u32[]{:S(2)}) %collective-permute-start) | collective-permute-done | bytes 1048608 | tf_op jit(solution)/shard_map/while/body/eval_jaxpr/ppermute | solution.py:13
  312.1 1.9 collective-permute-start
  314.0 20.3 %collective-permute-done = f32[2,16,64,128]{3,2,1,0:T(8,128)S(1)} collective-permute-done((f32[2,16,64,128]{3,2,1,0:T(8,128)S(1)}, f32[2,16,64,128]{3,2,1,0:T(8,128)S(1)}, u32[]{:S(2)}, u32[]{:S(2)}) %collective-permute-start) | collective-permute-done | bytes 1048608 | tf_op jit(solution)/shard_map/while/body/eval_jaxpr/ppermute | solution.py:13
  334.4 13.8 %multiply_reduce_fusion = (f32[4,256,2]{1,2,0:T(2,128)S(1)}, f32[4,256,2,16,64]{1,4,3,2,0:T(8,128)}) fusion(f32[4,256,2,16,64]{1,4,3,2,0:T(8,128)} %bitcast.164, bf16[4,256,2,16,64]{1,4,3,2,0:T(8,128)(2,1)} %bitcast.173, f32[2,16]{1,0:T(2,128)S(1)} %mul.128, f32[4,256,2,16]{1,3,2,0:T(8,128)S(1)} %bitcast_exponential_fusion, ...), kind=kOutput, calls=%fused_computation.43 | convolution fusion | flops 3252680704 | bytes 35267200 | tf_op jit(solution)/shard_map/ktgn,kghpn->ktghp/dot_general | solution.py:115
  348.1 13.8 %copy.127 = f32[4,256,2,16,64]{1,0,4,3,2:T(4,128)} copy(f32[4,256,2,16,64]{1,4,3,2,0:T(8,128)} %get-tuple-element.212) | data formatting | bytes 16777216 | tf_op jit(solution)/shard_map/convert_element_type | solution.py:41
  361.9 10.7 %reshape.130 = f32[1024,2,1024]{0,2,1:T(8,128)} reshape(f32[4,256,2,16,64]{1,0,4,3,2:T(4,128)} %copy.127) | data formatting | bytes 16777216 | tf_op jit(solution)/shard_map/convert_element_type | solution.py:41
  372.7 8.7 %copy.130 = f32[4,256,2,1024]{3,1,0,2:T(8,128)} copy(f32[4,256,2,1024]{1,3,2,0:T(8,128)} %bitcast.165) | data formatting | bytes 16777216 | tf_op jit(solution)/shard_map/convert_element_type | solution.py:41
  381.4 8.7 %copy.132 = f32[1024,2,1024]{0,2,1:T(8,128)} copy(f32[1024,2,1024]{2,0,1:T(8,128)} %bitcast.166) | data formatting | bytes 16777216 | tf_op jit(solution)/shard_map/convert_element_type | solution.py:41
  390.1 7.3 %multiply_convert_fusion.4 = bf16[1024,2,1024]{0,2,1:T(8,128)(2,1)S(1)} fusion(f32[1024,2,1024]{0,2,1:T(8,128)} %reshape.130, f32[1024,2,1024]{0,2,1:T(8,128)} %copy.132, f32[2,1024]{1,0:T(2,128)S(1)} %copy-done.1, f32[1024,2]{0,1:T(2,128)S(1)} %bitcast.180), kind=kLoop, calls=%fused_computation.42 | loop fusion | flops 16777216 | bytes 20987904 | tf_op jit(solution)/shard_map/convert_element_type | solution.py:43
  397.7 0.6 pad_maximum_fusion
  398.3 51.5 %all_to_all.86 = bf16[4,256,2,1024]{1,3,2,0:T(8,128)(2,1)} all-to-all(bf16[4,256,2,1024]{1,3,2,0:T(8,128)(2,1)S(1)} %pad_maximum_fusion), channel_id=1, replica_groups=mesh['seq'=8,'head'=4] {'head'}, dimensions={0} | all-to-all | bytes 8388608 | tf_op jit(solution)/shard_map/all_to_all | solution.py:136
  449.8 6.3 %copy.134 = bf16[256,8192]{1,0:T(8,128)(2,1)} copy(bf16[256,8192]{0,1:T(8,128)(2,1)} %bitcast.169) | data formatting | bytes 8388608 | tf_op jit(solution)/shard_map/reshape;reshape | solution.py:144
  (58 shorter events, 5.9 us)
Async XLA Ops:
  1.7 7.9 %all-to-all-start.3 = ((f32[256,8,16]{0,2,1:T(8,128)}), f32[256,8,16]{0,2,1:T(8,128)S(1)}, u32[]{:S(2)}, u32[]{:S(2)}) async-start(f32[256,8,16]{0,2,1:T(8,128)} %bitcast.22), calls=%async_computation.3 | async-start | bytes 262144 | tf_op jit(solution)/shard_map/all_to_all | solution.py:70
  9.6 7.9 %all-to-all-start.4 = ((f32[256,8,16]{0,2,1:T(8,128)}), f32[256,8,16]{0,2,1:T(8,128)S(1)}, u32[]{:S(2)}, u32[]{:S(2)}) async-start(f32[256,8,16]{0,2,1:T(8,128)} %bitcast.28), calls=%async_computation.4 | async-start | bytes 262144 | tf_op jit(solution)/shard_map/all_to_all | solution.py:69
  17.5 17.1 %all-to-all-start.1 = ((bf16[256,8,128]{2,0,1:T(8,128)(2,1)}), bf16[256,8,128]{2,0,1:T(8,128)(2,1)}, u32[]{:S(2)}, u32[]{:S(2)}) async-start(bf16[256,8,128]{2,0,1:T(8,128)(2,1)} %copy.117), calls=%async_computation.1 | async-start | bytes 1048576 | tf_op jit(solution)/shard_map/all_to_all | solution.py:66
  28.0 11.6 %copy-start = (bf16[256,8,128]{2,1,0:T(8,128)(2,1)S(1)}, bf16[256,8,128]{2,1,0:T(8,128)(2,1)}, u32[]{:S(2)}) copy-start(bf16[256,8,128]{2,1,0:T(8,128)(2,1)} %param.16) | copy-start | bytes 1572868
  34.5 12.3 %copy-start.2 = (f32[32]{0:T(128)S(1)}, f32[32]{0:T(128)}, u32[]{:S(2)}) copy-start(f32[32]{0:T(128)} %param.20) | copy-start | bytes 388
  34.5 53.2 %all-to-all-start = ((bf16[256,8,1024]{2,0,1:T(8,128)(2,1)}), bf16[256,8,1024]{2,0,1:T(8,128)(2,1)}, u32[]{:S(2)}, u32[]{:S(2)}) async-start(bf16[256,8,1024]{2,0,1:T(8,128)(2,1)} %copy.115), calls=%async_computation | async-start | bytes 8388608 | tf_op jit(solution)/shard_map/all_to_all | solution.py:63
  87.7 12.3 %all-to-all-start.2 = ((bf16[256,8,128]{2,0,1:T(8,128)(2,1)}), bf16[256,8,128]{2,0,1:T(8,128)(2,1)S(1)}, u32[]{:S(2)}, u32[]{:S(2)}) async-start(bf16[256,8,128]{2,0,1:T(8,128)(2,1)} %copy.118), calls=%async_computation.2 | async-start | bytes 1048576 | tf_op jit(solution)/shard_map/all_to_all | solution.py:65
  100.0 53.1 %all-to-all-start.5 = ((bf16[256,8,1024]{0,2,1:T(8,128)(2,1)}), bf16[256,8,1024]{0,2,1:T(8,128)(2,1)}, u32[]{:S(2)}, u32[]{:S(2)}) async-start(bf16[256,8,1024]{0,2,1:T(8,128)(2,1)} %bitcast.168), calls=%async_computation.5 | async-start | bytes 8388608 | tf_op jit(solution)/shard_map/all_to_all | solution.py:64
  159.5 27.4 %collective-permute-start = (f32[2,16,64,128]{3,2,1,0:T(8,128)S(1)}, f32[2,16,64,128]{3,2,1,0:T(8,128)S(1)}, u32[]{:S(2)}, u32[]{:S(2)}) collective-permute-start(f32[2,16,64,128]{3,2,1,0:T(8,128)S(1)} %multiply_add_fusion.2), channel_id=1, source_target_pairs={{0,4},{4,8},{8,12},{12,16},{16,20},{20,24},{24,28},{1,5},{5,9},{9,... | collective-permute-start | bytes 3145736 | tf_op jit(solution)/shard_map/while/body/eval_jaxpr/ppermute | solution.py:13
  187.1 26.5 %collective-permute-start = (f32[2,16,64,128]{3,2,1,0:T(8,128)S(1)}, f32[2,16,64,128]{3,2,1,0:T(8,128)S(1)}, u32[]{:S(2)}, u32[]{:S(2)}) collective-permute-start(f32[2,16,64,128]{3,2,1,0:T(8,128)S(1)} %multiply_add_fusion.2), channel_id=1, source_target_pairs={{0,4},{4,8},{8,12},{12,16},{16,20},{20,24},{24,28},{1,5},{5,9},{9,... | collective-permute-start | bytes 3145736 | tf_op jit(solution)/shard_map/while/body/eval_jaxpr/ppermute | solution.py:13
  213.8 25.7 %collective-permute-start = (f32[2,16,64,128]{3,2,1,0:T(8,128)S(1)}, f32[2,16,64,128]{3,2,1,0:T(8,128)S(1)}, u32[]{:S(2)}, u32[]{:S(2)}) collective-permute-start(f32[2,16,64,128]{3,2,1,0:T(8,128)S(1)} %multiply_add_fusion.2), channel_id=1, source_target_pairs={{0,4},{4,8},{8,12},{12,16},{16,20},{20,24},{24,28},{1,5},{5,9},{9,... | collective-permute-start | bytes 3145736 | tf_op jit(solution)/shard_map/while/body/eval_jaxpr/ppermute | solution.py:13
  239.6 24.8 %collective-permute-start = (f32[2,16,64,128]{3,2,1,0:T(8,128)S(1)}, f32[2,16,64,128]{3,2,1,0:T(8,128)S(1)}, u32[]{:S(2)}, u32[]{:S(2)}) collective-permute-start(f32[2,16,64,128]{3,2,1,0:T(8,128)S(1)} %multiply_add_fusion.2), channel_id=1, source_target_pairs={{0,4},{4,8},{8,12},{12,16},{16,20},{20,24},{24,28},{1,5},{5,9},{9,... | collective-permute-start | bytes 3145736 | tf_op jit(solution)/shard_map/while/body/eval_jaxpr/ppermute | solution.py:13
  264.6 24.0 %collective-permute-start = (f32[2,16,64,128]{3,2,1,0:T(8,128)S(1)}, f32[2,16,64,128]{3,2,1,0:T(8,128)S(1)}, u32[]{:S(2)}, u32[]{:S(2)}) collective-permute-start(f32[2,16,64,128]{3,2,1,0:T(8,128)S(1)} %multiply_add_fusion.2), channel_id=1, source_target_pairs={{0,4},{4,8},{8,12},{12,16},{16,20},{20,24},{24,28},{1,5},{5,9},{9,... | collective-permute-start | bytes 3145736 | tf_op jit(solution)/shard_map/while/body/eval_jaxpr/ppermute | solution.py:13
  288.8 23.2 %collective-permute-start = (f32[2,16,64,128]{3,2,1,0:T(8,128)S(1)}, f32[2,16,64,128]{3,2,1,0:T(8,128)S(1)}, u32[]{:S(2)}, u32[]{:S(2)}) collective-permute-start(f32[2,16,64,128]{3,2,1,0:T(8,128)S(1)} %multiply_add_fusion.2), channel_id=1, source_target_pairs={{0,4},{4,8},{8,12},{12,16},{16,20},{20,24},{24,28},{1,5},{5,9},{9,... | collective-permute-start | bytes 3145736 | tf_op jit(solution)/shard_map/while/body/eval_jaxpr/ppermute | solution.py:13
  312.1 22.3 %collective-permute-start = (f32[2,16,64,128]{3,2,1,0:T(8,128)S(1)}, f32[2,16,64,128]{3,2,1,0:T(8,128)S(1)}, u32[]{:S(2)}, u32[]{:S(2)}) collective-permute-start(f32[2,16,64,128]{3,2,1,0:T(8,128)S(1)} %multiply_add_fusion.2), channel_id=1, source_target_pairs={{0,4},{4,8},{8,12},{12,16},{16,20},{20,24},{24,28},{1,5},{5,9},{9,... | collective-permute-start | bytes 3145736 | tf_op jit(solution)/shard_map/while/body/eval_jaxpr/ppermute | solution.py:13
  381.4 8.7 %copy-start.1 = (f32[2,1024]{1,0:T(2,128)S(1)}, f32[2,1024]{1,0:T(2,128)}, u32[]{:S(2)}) copy-start(f32[2,1024]{1,0:T(2,128)} %mul.139) | copy-start | bytes 24580
